TPU v7x, 512 devices: a whole 4x4x16 slice. The times are simulated.
512 devices in a mesh: row: 16 (over z), col: 32 (over y, x, core).
Axes of the slice: x: 4, y: 4, z: 16, core: 2. Of those that a mesh axis runs over, the one named last changes fastest.
Arguments:
- new_keys: bfloat16 [1024, 28672], P('col', 'row'), may hold values from -6 to 6
- precision: bfloat16 [28672, 28672], P('row', 'col'), may hold values from -0.03125 to 0.03125
- stored_keys: bfloat16 [32, 256, 28672], P('row', None, 'col'), may hold values from -0.03125 to 0.03125
- pair_batch: int32 [16, 24], replicated, may hold values from 0 to 31, as said below
- pair_count: int32 [16], replicated, may hold values from 8 to 24, as said below
- batch_length: int32 [32], replicated, may hold values from 64 to 256
- batch_slot: int32 [32], replicated, may hold values from 0 to 31, each once
Outputs:
- whitened: bfloat16 [1024, 28672], P('row', 'col')
- intersections: float32 [16, 24, 64, 256], P('row', None, 'col')
Inputs may be any that keep to these rules, and one draw needn't show every extreme that they name: `pair_batch`: the ids in one block's row are distinct; ids at places at or beyond the block's count are ignored. `pair_count`: some block lists exactly 24 batches. `batch_slot`: every store slot belongs to exactly one batch.
All inputs are finite; a program needn't handle non-finite values.
Results may differ from a plain program's by a relative error of at most 0.0029.
Values may be sent and summed in bfloat16 or wider, within the bound.
A program may use at most 64 MiB of HBM per device.

v0:
```python
import jax
import jax.numpy as jnp
from jax import lax
from jax.sharding import PartitionSpec as P


def shards(new_keys, precision, stored_keys, pair_batch, pair_count, batch_length, batch_slot):
    row_count = lax.axis_size("row")
    col_count = lax.axis_size("col")
    row_index = lax.axis_index("row")
    total_keys = new_keys.shape[0] * col_count
    block_keys = total_keys // row_count
    part_keys = block_keys // col_count
    local_batches, batch_keys, width = stored_keys.shape
    partial_value = jnp.dot(
        lax.all_gather(new_keys, "col", axis=0, tiled=True),
        precision,
        preferred_element_type=jnp.float32,
    )
    summed = lax.psum_scatter(partial_value, "row", scatter_dimension=0, tiled=True)
    whitened = summed.astype(jnp.bfloat16)
    every_row = lax.all_gather(whitened, "row", axis=0, tiled=True)
    rows = every_row.reshape(row_count, col_count, part_keys, width)
    terms = jnp.einsum("bcid,sjd->csbij", rows, stored_keys, preferred_element_type=jnp.float32)
    mine = lax.psum_scatter(terms, "col", scatter_dimension=0, tiled=True)[0]
    routed = lax.all_to_all(mine, "row", split_axis=1, concat_axis=0, tiled=True)
    table = routed[:, 0]
    listed = pair_batch[row_index]
    slots = batch_slot[listed]
    lengths = batch_length[listed]
    count = pair_count[row_index]
    picked = jnp.take(table, slots, axis=0)
    places = jnp.arange(slots.shape[0], dtype=jnp.int32)
    columns = jnp.arange(batch_keys, dtype=jnp.int32)
    keep = (places < count)[:, None, None] & (columns[None, None, :] < lengths[:, None, None])
    shares = jnp.where(keep, picked, jnp.zeros_like(picked))
    return (whitened, shares[None])


def solution(mesh):
    placed = (P("col", "row"), P("row", "col"), P("row", None, "col"), P(), P(), P(), P())
    return jax.shard_map(
        shards,
        mesh=mesh,
        in_specs=placed,
        out_specs=(P("row", "col"), P("row", None, "col", None)),
        check_vma=False,
    )
```

profile of v0, /device:TPU:6, one launch (start us, length us, event | category | flops | bytes accessed | tf_op | source)
XLA Modules:
  0.0 379.6 jit_solution(4652722605744629083)
XLA Ops:
  7.2 0.7 all-gather.3.cloned.1.call-update
  7.9 0.0 reduce-scatter.3.cloned.1.call-start
  8.0 68.1 %all-gather.3.cloned.1.call-done = bf16[1024,1792]{1,0:T(8,128)(2,1)} async-done(((bf16[32,1792]{1,0:T(8,128)(2,1)}), bf16[1024,1792]{1,0:T(8,128)(2,1)}) %all-gather.3.cloned.1.call-update) | async-done | bytes 3670032 | tf_op jit(solution)/shard_map/all_gather | solution.py:16
  76.0 7.8 %fusion.10 = f32[1024,896]{1,0:T(8,128)} fusion(bf16[1024,1792]{1,0:T(8,128)(2,1)} %all-gather.3.cloned.1.call-done, bf16[1792,896]{1,0:T(8,128)(2,1)S(1)} %copy-done), kind=kOutput, calls=%fused_computation.20 | convolution fusion | flops 3288334336 | bytes 10551296 | tf_op jit(solution)/shard_map/dot_general | solution.py:15
  83.8 0.0 all-gather.5.cloned.1.call-start
  83.9 78.2 %reduce-scatter.3.cloned.1.call-done = f32[64,896]{1,0:T(8,128)} async-done(((f32[1024,896]{1,0:T(8,128)}), f32[64,896]{1,0:T(8,128)}) %reduce-scatter.3.cloned.1.call-update) | async-done | bytes 229392 | tf_op jit(solution)/shard_map/reduce_scatter | solution.py:20
  162.1 1.6 convert_element_type.3
  163.7 0.0 reduce-scatter.5.cloned.1.call-start
  163.8 72.0 %all-gather.5.cloned.1.call-done = bf16[1024,896]{1,0:T(8,128)(2,1)} async-done(((bf16[64,896]{1,0:T(8,128)(2,1)}), bf16[1024,896]{1,0:T(8,128)(2,1)}) %all-gather.5.cloned.1.call-update) | async-done | bytes 1835024 | tf_op jit(solution)/shard_map/all_gather | solution.py:22
  235.8 4.8 %reshape.105 = bf16[16,32,2,896]{3,2,1,0:T(2,128)(2,1)} reshape(bf16[1024,896]{1,0:T(8,128)(2,1)} %all-gather.5.cloned.1.call-done) | data formatting | bytes 3670016 | tf_op jit(solution)/shard_map/reshape | solution.py:23
  240.7 3.0 fusion.2
  243.7 2.5 copy.16
  246.3 0.6 dynamic_slice.6
  246.9 0.7 fusion.8
  247.6 0.7 gather_fusion.1
  248.3 96.7 %reduce-scatter.5.cloned.1.call-done = f32[1,2,16,2,256]{4,2,3,1,0:T(8,128)} async-done(((f32[32,2,16,2,256]{4,2,3,1,0:T(8,128)}), f32[1,2,16,2,256]{4,2,3,1,0:T(8,128)}) %reduce-scatter.5.cloned.1.call-update) | async-done | bytes 65552 | tf_op jit(solution)/shard_map/reduce_scatter | solution.py:25
  345.1 1.5 copy.17
  346.6 12.3 %all-to-all-start = ((f32[2,16,2,256]{3,2,0,1:T(2,128)}), f32[2,16,2,256]{3,2,0,1:T(2,128)S(1)}, u32[]{:S(2)}, u32[]{:S(2)}) async-start(f32[2,16,2,256]{3,2,0,1:T(2,128)} %copy.17), calls=%async_computation.2 | async-start | bytes 131072 | tf_op jit(solution)/shard_map/all_to_all | solution.py:26
  358.9 0.7 iota_compare_fusion.1
  359.6 0.7 gather_fusion
  360.3 0.1 fusion.7
  360.4 11.4 %all-to-all-done = f32[2,16,2,256]{3,2,0,1:T(2,128)S(1)} async-done(((f32[2,16,2,256]{3,2,0,1:T(2,128)}), f32[2,16,2,256]{3,2,0,1:T(2,128)S(1)}, u32[]{:S(2)}, u32[]{:S(2)}) %all-to-all-start) | async-done | bytes 65568 | tf_op jit(solution)/shard_map/all_to_all | solution.py:26
  371.8 0.6 gather_fusion.2
  372.4 0.7 fusion.6
  (16 shorter events, 0.1 us)
Async XLA Ops:
  7.2 68.9 %copy-start = (bf16[1792,896]{1,0:T(8,128)(2,1)S(1)}, bf16[1792,896]{1,0:T(8,128)(2,1)}, u32[]{:S(2)}) copy-start(bf16[1792,896]{1,0:T(8,128)(2,1)} %param.8) | copy-start | bytes 9633796
  7.2 68.9 %all-gather.3.cloned.1.call-start = ((), (), s32[]{:S(2)}) async-start(), calls=%async_computation.3 | async-start | bytes 3784704 | tf_op jit(solution)/shard_map/all_gather | solution.py:16
  7.9 154.2 %reduce-scatter.3.cloned.1.call-start = ((), (), s32[]{:S(2)}) async-start(), calls=%async_computation.4 | async-start | bytes 3899392 | tf_op jit(solution)/shard_map/reduce_scatter | solution.py:20
  83.8 152.0 %all-gather.5.cloned.1.call-start = ((), (), s32[]{:S(2)}) async-start(), calls=%async_computation.5 | async-start | bytes 1949696 | tf_op jit(solution)/shard_map/all_gather | solution.py:22
  163.7 181.3 %reduce-scatter.5.cloned.1.call-start = ((), (), s32[]{:S(2)}) async-start(), calls=%async_computation.6 | async-start | bytes 2162688 | tf_op jit(solution)/shard_map/reduce_scatter | solution.py:25
  243.7 2.6 copy-start.3
  243.7 3.9 %copy-start.1 = (s32[32]{0:T(128)S(1)}, s32[32]{0:T(128)}, u32[]{:S(2)}) copy-start(s32[32]{0:T(128)} %param.13) | copy-start | bytes 388
  243.7 115.9 %copy-start.2 = (s32[32]{0:T(128)S(1)}, s32[32]{0:T(128)}, u32[]{:S(2)}) copy-start(s32[32]{0:T(128)} %param.12) | copy-start | bytes 388
  346.6 25.2 %all-to-all-start = ((f32[2,16,2,256]{3,2,0,1:T(2,128)}), f32[2,16,2,256]{3,2,0,1:T(2,128)S(1)}, u32[]{:S(2)}, u32[]{:S(2)}) async-start(f32[2,16,2,256]{3,2,0,1:T(2,128)} %copy.17), calls=%async_computation.2 | async-start | bytes 131072 | tf_op jit(solution)/shard_map/all_to_all | solution.py:26
Sparse Core Ops, SparseCore 0:
  11.1 64.8 all-gather.2
  84.0 78.1 reduce-scatter.2
  164.8 71.0 all-gather.4
  246.4 98.6 reduce-scatter.4
where the time goes:
time: 380 us
  waiting for transfers between devices  327 us (86%)
  between operations  13.9 us (4%)
  starting transfers between devices  12.5 us (3%)
  local copies, waits for them, and re-layouts  11.5 us (3%)
  matrix products  10.8 us (3%)
    reduce_scatter x1, waiting for transfers between devices, shards(): mine = lax.psum_scatter(terms, 'col', scatter_dimension=0, tiled=True)[0]  96.7 us
    reduce_scatter x1, waiting for transfers between devices, shards(): lax.psum_scatter(partial_value, 'row', scatter_dimension=0, tiled=True)  78.2 us
    all_gather x1, waiting for transfers between devices, shards(): every_row = lax.all_gather(whitened, 'row', axis=0, tiled=True)  72 us
    all_gather x1, waiting for transfers between devices, shards(): lax.all_gather(new_keys, 'col', axis=0, tiled=True)  68.1 us
    all_to_all x1, starting transfers between devices, shards(): lax.all_to_all(mine, 'row', split_axis=1, concat_axis=0, tiled=True)  12.3 us
    all_to_all x1, waiting for transfers between devices, shards(): lax.all_to_all(mine, 'row', split_axis=1, concat_axis=0, tiled=True)  11.4 us
    dot_general x1, matrix products, shards(): jnp.dot(lax.all_gather(new_keys, 'col', axis=0, tiled=True), precision, p...  7.77 us
  transfers between devices with their start and end apart: 5, of which 5 were waited for; matrix products, arithmetic and copies ran while one was open for 1% of the time, Pallas kernels for 0%

commit v1 on v0

--- a/solution.py
+++ b/solution.py
@@ -2,6 +2,18 @@
 import jax.numpy as jnp
 from jax import lax
 from jax.sharding import PartitionSpec as P
+
+
+def cut_along(shard, dim, peers):
+    dims = shard.shape
+    blocks = shard.reshape(*dims[:dim], peers, dims[dim] // peers, *dims[dim + 1 :])
+    return jnp.moveaxis(blocks, dim, 0)
+
+
+def in_order(parts, dim):
+    dims = list(parts.shape[1:])
+    dims[dim] *= parts.shape[0]
+    return jnp.moveaxis(parts, 0, dim).reshape(dims)
 
 
 def shards(new_keys, precision, stored_keys, pair_batch, pair_count, batch_length, batch_slot):
@@ -23,7 +35,14 @@
     rows = every_row.reshape(row_count, col_count, part_keys, width)
     terms = jnp.einsum("bcid,sjd->csbij", rows, stored_keys, preferred_element_type=jnp.float32)
     mine = lax.psum_scatter(terms, "col", scatter_dimension=0, tiled=True)[0]
-    routed = lax.all_to_all(mine, "row", split_axis=1, concat_axis=0, tiled=True)
+    length, index = (lax.axis_size("row"), lax.axis_index("row"))
+    blocks = cut_along(mine, 1, length)
+    gathered = [blocks[index]]
+    for turn in range(1, length):
+        sent = blocks[index ^ turn]
+        gathered.append(lax.ppermute(sent, "row", [(i, i ^ turn) for i in range(length)]))
+    blocks = jnp.stack(gathered)[index ^ jnp.arange(length)]
+    routed = in_order(blocks, 0)
     table = routed[:, 0]
     listed = pair_batch[row_index]
     slots = batch_slot[listed]

time: 380 us -> 440 us (1.16)
  starting transfers between devices: 12.5 us -> 76.5 us
  waiting for transfers between devices: 327 us -> 319 us
    ppermute x0 -> x15, starting transfers between devices: none -> 76.4 us  [shards(): lax.ppermute(sent, 'row', [(i, i ^ turn) for i in range(length)])]
    all_to_all x1 -> x0, starting transfers between devices: 12.3 us -> none  [shards(): lax.all_to_all(mine, 'row', split_axis=1, concat_axis=0, tiled=True)]
    all_to_all x1 -> x0, waiting for transfers between devices: 11.4 us -> none  [shards(): lax.all_to_all(mine, 'row', split_axis=1, concat_axis=0, tiled=True)]
    ppermute x0 -> x15, waiting for transfers between devices: none -> 4.72 us  [shards(): lax.ppermute(sent, 'row', [(i, i ^ turn) for i in range(length)])]
  transfers between devices with their start and end apart: 5 -> 19, of which waited for: 5 -> 5; matrix products, arithmetic and copies ran while one was open for 1% -> 1% of each run, Pallas kernels for 0% -> 0%
where the time goes in v1:
time: 440 us; the launch traced here: 437 us
  waiting for transfers between devices  319 us (72%)
  starting transfers between devices  76.5 us (17%)
  between operations  14.3 us (3%)
  local copies, waits for them, and re-layouts  12.4 us (3%)
  matrix products  10.8 us (2%)
    reduce_scatter x1, waiting for transfers between devices, shards(): mine = lax.psum_scatter(terms, 'col', scatter_dimension=0, tiled=True)[0]  95.2 us
    reduce_scatter x1, waiting for transfers between devices, shards(): lax.psum_scatter(partial_value, 'row', scatter_dimension=0, tiled=True)  78.2 us
    ppermute x15, starting transfers between devices, shards(): lax.ppermute(sent, 'row', [(i, i ^ turn) for i in range(length)])  76.4 us
    all_gather x1, waiting for transfers between devices, shards(): every_row = lax.all_gather(whitened, 'row', axis=0, tiled=True)  72 us
    all_gather x1, waiting for transfers between devices, shards(): lax.all_gather(new_keys, 'col', axis=0, tiled=True)  68.1 us
  transfers between devices with their start and end apart: 19, of which 5 were waited for; matrix products, arithmetic and copies ran while one was open for 1% of the time, Pallas kernels for 0%

profile of v1, /device:TPU:6, one launch (start us, length us, event | category | flops | bytes accessed | tf_op | source)
XLA Modules:
  0.0 436.8 jit_solution(4665073949928509452)
XLA Ops:
  8.0 68.1 %all-gather.3.cloned.1.call-done = bf16[1024,1792]{1,0:T(8,128)(2,1)} async-done(((bf16[32,1792]{1,0:T(8,128)(2,1)}), bf16[1024,1792]{1,0:T(8,128)(2,1)}) %all-gather.3.cloned.1.call-update) | async-done | bytes 3670032 | tf_op jit(solution)/shard_map/all_gather | solution.py:28
  76.0 7.8 %fusion.12 = f32[1024,896]{1,0:T(8,128)} fusion(bf16[1024,1792]{1,0:T(8,128)(2,1)} %all-gather.3.cloned.1.call-done, bf16[1792,896]{1,0:T(8,128)(2,1)S(1)} %copy-done), kind=kOutput, calls=%fused_computation.73 | convolution fusion | flops 3288334336 | bytes 10551296 | tf_op jit(solution)/shard_map/dot_general | solution.py:27
  83.9 78.2 %reduce-scatter.3.cloned.1.call-done = f32[64,896]{1,0:T(8,128)} async-done(((f32[1024,896]{1,0:T(8,128)}), f32[64,896]{1,0:T(8,128)}) %reduce-scatter.3.cloned.1.call-update) | async-done | bytes 229392 | tf_op jit(solution)/shard_map/reduce_scatter | solution.py:32
  163.8 72.0 %all-gather.5.cloned.1.call-done = bf16[1024,896]{1,0:T(8,128)(2,1)} async-done(((bf16[64,896]{1,0:T(8,128)(2,1)}), bf16[1024,896]{1,0:T(8,128)(2,1)}) %all-gather.5.cloned.1.call-update) | async-done | bytes 1835024 | tf_op jit(solution)/shard_map/all_gather | solution.py:34
  235.8 4.8 %reshape.183 = bf16[16,32,2,896]{3,2,1,0:T(2,128)(2,1)} reshape(bf16[1024,896]{1,0:T(8,128)(2,1)} %all-gather.5.cloned.1.call-done) | data formatting | bytes 3670016 | tf_op jit(solution)/shard_map/reshape | solution.py:35
  240.6 3.0 fusion.2
  243.7 2.5 copy.13
  249.8 95.2 %reduce-scatter.5.cloned.1.call-done = f32[1,2,16,2,256]{4,2,3,1,0:T(8,128)} async-done(((f32[32,2,16,2,256]{4,2,3,1,0:T(8,128)}), f32[1,2,16,2,256]{4,2,3,1,0:T(8,128)}) %reduce-scatter.5.cloned.1.call-update) | async-done | bytes 65552 | tf_op jit(solution)/shard_map/reduce_scatter | solution.py:37
  346.6 3.5 collective-permute-start
  350.1 4.5 %collective-permute-start.1 = (f32[2,1,2,256]{3,2,0,1:T(2,128)S(1)}, f32[2,1,2,256]{3,2,0,1:T(2,128)S(1)}, u32[]{:S(2)}, u32[]{:S(2)}) collective-permute-start(f32[2,1,2,256]{3,2,0,1:T(2,128)S(1)} %bitcast.120), channel_id=1, source_target_pairs={{0,64},{32,96},{64,0},{96,32},{128,192},{160,224},{192,128},{224,1... | collective-permute-start | bytes 12296 | tf_op jit(solution)/shard_map/ppermute | solution.py:43
  354.6 2.2 collective-permute-start.2
  356.8 7.7 %collective-permute-start.3 = (f32[2,1,2,256]{3,2,0,1:T(2,128)S(1)}, f32[2,1,2,256]{3,2,0,1:T(2,128)S(1)}, u32[]{:S(2)}, u32[]{:S(2)}) collective-permute-start(f32[2,1,2,256]{3,2,0,1:T(2,128)S(1)} %bitcast.118), channel_id=1, source_target_pairs={{0,128},{32,160},{64,192},{96,224},{128,0},{160,32},{192,64},{224,... | collective-permute-start | bytes 12296 | tf_op jit(solution)/shard_map/ppermute | solution.py:43
  364.5 2.2 collective-permute-start.4
  366.8 9.7 %collective-permute-start.5 = (f32[2,1,2,256]{3,2,0,1:T(2,128)S(1)}, f32[2,1,2,256]{3,2,0,1:T(2,128)S(1)}, u32[]{:S(2)}, u32[]{:S(2)}) collective-permute-start(f32[2,1,2,256]{3,2,0,1:T(2,128)S(1)} %bitcast.116), channel_id=1, source_target_pairs={{0,192},{32,224},{64,128},{96,160},{128,64},{160,96},{192,0},{224,... | collective-permute-start | bytes 12296 | tf_op jit(solution)/shard_map/ppermute | solution.py:43
  376.5 1.9 collective-permute-start.6
  378.5 12.7 %collective-permute-start.7 = (f32[2,1,2,256]{3,2,0,1:T(2,128)S(1)}, f32[2,1,2,256]{3,2,0,1:T(2,128)S(1)}, u32[]{:S(2)}, u32[]{:S(2)}) collective-permute-start(f32[2,1,2,256]{3,2,0,1:T(2,128)S(1)} %bitcast.114), channel_id=1, source_target_pairs={{0,256},{32,288},{64,320},{96,352},{128,384},{160,416},{192,448},{... | collective-permute-start | bytes 12296 | tf_op jit(solution)/shard_map/ppermute | solution.py:43
  391.2 1.9 collective-permute-start.8
  393.1 6.6 %collective-permute-start.9 = (f32[2,1,2,256]{3,2,0,1:T(2,128)S(1)}, f32[2,1,2,256]{3,2,0,1:T(2,128)S(1)}, u32[]{:S(2)}, u32[]{:S(2)}) collective-permute-start(f32[2,1,2,256]{3,2,0,1:T(2,128)S(1)} %bitcast.112), channel_id=1, source_target_pairs={{0,320},{32,352},{64,256},{96,288},{128,448},{160,480},{192,384},{... | collective-permute-start | bytes 12296 | tf_op jit(solution)/shard_map/ppermute | solution.py:43
  399.8 5.2 %collective-permute-start.10 = (f32[2,1,2,256]{3,2,0,1:T(2,128)S(1)}, f32[2,1,2,256]{3,2,0,1:T(2,128)S(1)}, u32[]{:S(2)}, u32[]{:S(2)}) collective-permute-start(f32[2,1,2,256]{3,2,0,1:T(2,128)S(1)} %bitcast.111), channel_id=1, source_target_pairs={{0,352},{32,320},{64,288},{96,256},{128,480},{160,448},{192,416},{... | collective-permute-start | bytes 12296 | tf_op jit(solution)/shard_map/ppermute | solution.py:43
  405.1 5.1 %collective-permute-start.11 = (f32[2,1,2,256]{3,2,0,1:T(2,128)S(1)}, f32[2,1,2,256]{3,2,0,1:T(2,128)S(1)}, u32[]{:S(2)}, u32[]{:S(2)}) collective-permute-start(f32[2,1,2,256]{3,2,0,1:T(2,128)S(1)} %bitcast.110), channel_id=1, source_target_pairs={{0,384},{32,416},{64,448},{96,480},{128,256},{160,288},{192,320},{... | collective-permute-start | bytes 12296 | tf_op jit(solution)/shard_map/ppermute | solution.py:43
  410.2 5.5 %collective-permute-start.12 = (f32[2,1,2,256]{3,2,0,1:T(2,128)S(1)}, f32[2,1,2,256]{3,2,0,1:T(2,128)S(1)}, u32[]{:S(2)}, u32[]{:S(2)}) collective-permute-start(f32[2,1,2,256]{3,2,0,1:T(2,128)S(1)} %bitcast.109), channel_id=1, source_target_pairs={{0,416},{32,384},{64,480},{96,448},{128,288},{160,256},{192,352},{... | collective-permute-start | bytes 12296 | tf_op jit(solution)/shard_map/ppermute | solution.py:43
  415.8 5.8 %collective-permute-start.13 = (f32[2,1,2,256]{3,2,0,1:T(2,128)S(1)}, f32[2,1,2,256]{3,2,0,1:T(2,128)S(1)}, u32[]{:S(2)}, u32[]{:S(2)}) collective-permute-start(f32[2,1,2,256]{3,2,0,1:T(2,128)S(1)} %bitcast.108), channel_id=1, source_target_pairs={{0,448},{32,480},{64,384},{96,416},{128,320},{160,352},{192,256},{... | collective-permute-start | bytes 12296 | tf_op jit(solution)/shard_map/ppermute | solution.py:43
  421.6 1.9 collective-permute-start.14
  423.6 4.7 %collective-permute-done.14 = f32[2,1,2,256]{3,2,0,1:T(2,128)S(1)} collective-permute-done((f32[2,1,2,256]{3,2,0,1:T(2,128)S(1)}, f32[2,1,2,256]{3,2,0,1:T(2,128)S(1)}, u32[]{:S(2)}, u32[]{:S(2)}) %collective-permute-start.14) | collective-permute-done | bytes 4128 | tf_op jit(solution)/shard_map/ppermute | solution.py:43
  (78 shorter events, 9.7 us)
Async XLA Ops:
  7.2 68.9 %copy-start = (bf16[1792,896]{1,0:T(8,128)(2,1)S(1)}, bf16[1792,896]{1,0:T(8,128)(2,1)}, u32[]{:S(2)}) copy-start(bf16[1792,896]{1,0:T(8,128)(2,1)} %param.8) | copy-start | bytes 9633796
  7.2 68.9 %all-gather.3.cloned.1.call-start = ((), (), s32[]{:S(2)}) async-start(), calls=%async_computation.2 | async-start | bytes 3784704 | tf_op jit(solution)/shard_map/all_gather | solution.py:28
  7.9 154.2 %reduce-scatter.3.cloned.1.call-start = ((), (), s32[]{:S(2)}) async-start(), calls=%async_computation.3 | async-start | bytes 3899392 | tf_op jit(solution)/shard_map/reduce_scatter | solution.py:32
  83.8 152.0 %all-gather.5.cloned.1.call-start = ((), (), s32[]{:S(2)}) async-start(), calls=%async_computation.4 | async-start | bytes 1949696 | tf_op jit(solution)/shard_map/all_gather | solution.py:34
  163.7 181.3 %reduce-scatter.5.cloned.1.call-start = ((), (), s32[]{:S(2)}) async-start(), calls=%async_computation.5 | async-start | bytes 2162688 | tf_op jit(solution)/shard_map/reduce_scatter | solution.py:37
  243.7 3.4 copy-start.1
  243.7 4.1 copy-start.2
  243.7 4.8 %copy-start.3 = (s32[16]{0:T(128)S(1)}, s32[16]{0:T(128)}, u32[]{:S(2)}) copy-start(s32[16]{0:T(128)} %param.11) | copy-start | bytes 196
  346.6 20.2 %collective-permute-start = (f32[2,1,2,256]{3,2,0,1:T(2,128)S(1)}, f32[2,1,2,256]{3,2,0,1:T(2,128)S(1)}, u32[]{:S(2)}, u32[]{:S(2)}) collective-permute-start(f32[2,1,2,256]{3,2,0,1:T(2,128)S(1)} %bitcast.121), channel_id=1, source_target_pairs={{0,32},{32,0},{64,96},{96,64},{128,160},{160,128},{192,224},{224,1... | collective-permute-start | bytes 12296 | tf_op jit(solution)/shard_map/ppermute | solution.py:43
  350.1 26.4 %collective-permute-start.1 = (f32[2,1,2,256]{3,2,0,1:T(2,128)S(1)}, f32[2,1,2,256]{3,2,0,1:T(2,128)S(1)}, u32[]{:S(2)}, u32[]{:S(2)}) collective-permute-start(f32[2,1,2,256]{3,2,0,1:T(2,128)S(1)} %bitcast.120), channel_id=1, source_target_pairs={{0,64},{32,96},{64,0},{96,32},{128,192},{160,224},{192,128},{224,1... | collective-permute-start | bytes 12296 | tf_op jit(solution)/shard_map/ppermute | solution.py:43
  354.6 23.8 %collective-permute-start.2 = (f32[2,1,2,256]{3,2,0,1:T(2,128)S(1)}, f32[2,1,2,256]{3,2,0,1:T(2,128)S(1)}, u32[]{:S(2)}, u32[]{:S(2)}) collective-permute-start(f32[2,1,2,256]{3,2,0,1:T(2,128)S(1)} %bitcast.119), channel_id=1, source_target_pairs={{0,96},{32,64},{64,32},{96,0},{128,224},{160,192},{192,160},{224,1... | collective-permute-start | bytes 12296 | tf_op jit(solution)/shard_map/ppermute | solution.py:43
  356.8 34.4 %collective-permute-start.3 = (f32[2,1,2,256]{3,2,0,1:T(2,128)S(1)}, f32[2,1,2,256]{3,2,0,1:T(2,128)S(1)}, u32[]{:S(2)}, u32[]{:S(2)}) collective-permute-start(f32[2,1,2,256]{3,2,0,1:T(2,128)S(1)} %bitcast.118), channel_id=1, source_target_pairs={{0,128},{32,160},{64,192},{96,224},{128,0},{160,32},{192,64},{224,... | collective-permute-start | bytes 12296 | tf_op jit(solution)/shard_map/ppermute | solution.py:43
  364.5 28.6 %collective-permute-start.4 = (f32[2,1,2,256]{3,2,0,1:T(2,128)S(1)}, f32[2,1,2,256]{3,2,0,1:T(2,128)S(1)}, u32[]{:S(2)}, u32[]{:S(2)}) collective-permute-start(f32[2,1,2,256]{3,2,0,1:T(2,128)S(1)} %bitcast.117), channel_id=1, source_target_pairs={{0,160},{32,128},{64,224},{96,192},{128,32},{160,0},{192,96},{224,... | collective-permute-start | bytes 12296 | tf_op jit(solution)/shard_map/ppermute | solution.py:43
  366.8 33.0 %collective-permute-start.5 = (f32[2,1,2,256]{3,2,0,1:T(2,128)S(1)}, f32[2,1,2,256]{3,2,0,1:T(2,128)S(1)}, u32[]{:S(2)}, u32[]{:S(2)}) collective-permute-start(f32[2,1,2,256]{3,2,0,1:T(2,128)S(1)} %bitcast.116), channel_id=1, source_target_pairs={{0,192},{32,224},{64,128},{96,160},{128,64},{160,96},{192,0},{224,... | collective-permute-start | bytes 12296 | tf_op jit(solution)/shard_map/ppermute | solution.py:43
  376.5 28.5 %collective-permute-start.6 = (f32[2,1,2,256]{3,2,0,1:T(2,128)S(1)}, f32[2,1,2,256]{3,2,0,1:T(2,128)S(1)}, u32[]{:S(2)}, u32[]{:S(2)}) collective-permute-start(f32[2,1,2,256]{3,2,0,1:T(2,128)S(1)} %bitcast.115), channel_id=1, source_target_pairs={{0,224},{32,192},{64,160},{96,128},{128,96},{160,64},{192,32},{224... | collective-permute-start | bytes 12296 | tf_op jit(solution)/shard_map/ppermute | solution.py:43
  378.5 31.7 %collective-permute-start.7 = (f32[2,1,2,256]{3,2,0,1:T(2,128)S(1)}, f32[2,1,2,256]{3,2,0,1:T(2,128)S(1)}, u32[]{:S(2)}, u32[]{:S(2)}) collective-permute-start(f32[2,1,2,256]{3,2,0,1:T(2,128)S(1)} %bitcast.114), channel_id=1, source_target_pairs={{0,256},{32,288},{64,320},{96,352},{128,384},{160,416},{192,448},{... | collective-permute-start | bytes 12296 | tf_op jit(solution)/shard_map/ppermute | solution.py:43
  391.2 24.6 %collective-permute-start.8 = (f32[2,1,2,256]{3,2,0,1:T(2,128)S(1)}, f32[2,1,2,256]{3,2,0,1:T(2,128)S(1)}, u32[]{:S(2)}, u32[]{:S(2)}) collective-permute-start(f32[2,1,2,256]{3,2,0,1:T(2,128)S(1)} %bitcast.113), channel_id=1, source_target_pairs={{0,288},{32,256},{64,352},{96,320},{128,416},{160,384},{192,480},{... | collective-permute-start | bytes 12296 | tf_op jit(solution)/shard_map/ppermute | solution.py:43
  393.1 28.5 %collective-permute-start.9 = (f32[2,1,2,256]{3,2,0,1:T(2,128)S(1)}, f32[2,1,2,256]{3,2,0,1:T(2,128)S(1)}, u32[]{:S(2)}, u32[]{:S(2)}) collective-permute-start(f32[2,1,2,256]{3,2,0,1:T(2,128)S(1)} %bitcast.112), channel_id=1, source_target_pairs={{0,320},{32,352},{64,256},{96,288},{128,448},{160,480},{192,384},{... | collective-permute-start | bytes 12296 | tf_op jit(solution)/shard_map/ppermute | solution.py:43
  399.8 23.7 %collective-permute-start.10 = (f32[2,1,2,256]{3,2,0,1:T(2,128)S(1)}, f32[2,1,2,256]{3,2,0,1:T(2,128)S(1)}, u32[]{:S(2)}, u32[]{:S(2)}) collective-permute-start(f32[2,1,2,256]{3,2,0,1:T(2,128)S(1)} %bitcast.111), channel_id=1, source_target_pairs={{0,352},{32,320},{64,288},{96,256},{128,480},{160,448},{192,416},{... | collective-permute-start | bytes 12296 | tf_op jit(solution)/shard_map/ppermute | solution.py:43
  405.1 18.5 %collective-permute-start.11 = (f32[2,1,2,256]{3,2,0,1:T(2,128)S(1)}, f32[2,1,2,256]{3,2,0,1:T(2,128)S(1)}, u32[]{:S(2)}, u32[]{:S(2)}) collective-permute-start(f32[2,1,2,256]{3,2,0,1:T(2,128)S(1)} %bitcast.110), channel_id=1, source_target_pairs={{0,384},{32,416},{64,448},{96,480},{128,256},{160,288},{192,320},{... | collective-permute-start | bytes 12296 | tf_op jit(solution)/shard_map/ppermute | solution.py:43
  410.2 13.4 %collective-permute-start.12 = (f32[2,1,2,256]{3,2,0,1:T(2,128)S(1)}, f32[2,1,2,256]{3,2,0,1:T(2,128)S(1)}, u32[]{:S(2)}, u32[]{:S(2)}) collective-permute-start(f32[2,1,2,256]{3,2,0,1:T(2,128)S(1)} %bitcast.109), channel_id=1, source_target_pairs={{0,416},{32,384},{64,480},{96,448},{128,288},{160,256},{192,352},{... | collective-permute-start | bytes 12296 | tf_op jit(solution)/shard_map/ppermute | solution.py:43
  415.8 7.8 %collective-permute-start.13 = (f32[2,1,2,256]{3,2,0,1:T(2,128)S(1)}, f32[2,1,2,256]{3,2,0,1:T(2,128)S(1)}, u32[]{:S(2)}, u32[]{:S(2)}) collective-permute-start(f32[2,1,2,256]{3,2,0,1:T(2,128)S(1)} %bitcast.108), channel_id=1, source_target_pairs={{0,448},{32,480},{64,384},{96,416},{128,320},{160,352},{192,256},{... | collective-permute-start | bytes 12296 | tf_op jit(solution)/shard_map/ppermute | solution.py:43
  421.6 6.7 %collective-permute-start.14 = (f32[2,1,2,256]{3,2,0,1:T(2,128)S(1)}, f32[2,1,2,256]{3,2,0,1:T(2,128)S(1)}, u32[]{:S(2)}, u32[]{:S(2)}) collective-permute-start(f32[2,1,2,256]{3,2,0,1:T(2,128)S(1)} %bitcast.107), channel_id=1, source_target_pairs={{0,480},{32,448},{64,416},{96,384},{128,352},{160,320},{192,288},{... | collective-permute-start | bytes 12296 | tf_op jit(solution)/shard_map/ppermute | solution.py:43
Sparse Core Ops, SparseCore 0:
  11.1 64.8 all-gather.2
  84.0 78.1 reduce-scatter.2
  164.8 71.0 all-gather.4
  246.4 98.6 reduce-scatter.4
